TPU v7x, 256 devices: a whole 4x4x8 slice. The times are simulated.
256 devices in a mesh: video: 4 (over x), tm: 16 (over z, core), space: 4 (over y).
Axes of the slice: x: 4, y: 4, z: 8, core: 2. Of those that a mesh axis runs over, the one named last changes fastest.
Arguments:
- feature_maps: bfloat16 [64, 128, 240, 128], P(('video', 'tm'), 'space'), parts along dimension 0, may hold values from -27 to 27
- query_frame: int32 [2048], P('video'), parts along dimension 0, may hold values from 0 to 15
- query_row: int32 [2048], P('video'), parts along dimension 0, may hold values from 0 to 127
- query_col: int32 [2048], P('video'), parts along dimension 0, may hold values from 0 to 239
- ema_decay: float32 [64, 128], P(('video', 'tm')), parts along dimension 0, may hold values from 0.14 to 1
- dw_kernel: float32 [3, 128], replicated, may hold values from -3 to 3
- pw_weight: bfloat16 [128, 128], replicated, may hold values from -0.5 to 0.5
- out_weight: float32 [2, 128], replicated, may hold values from -2 to 2
Outputs:
- tracks: float32 [64, 2, 512], P(('video', 'tm')), parts along dimension 0
There are 4 independent parts, one for each index of `video`. A program takes and returns all parts, laid end to end along the dimension named above; an argument that names none is the same for every part. Nothing has to cross between parts.
All inputs are finite; a program needn't handle non-finite values.
Results may differ from a plain program's by a relative error of at most 0.0026.
Values may be sent and summed in bfloat16 or wider, within the bound.
A program may use at most 128 MiB of HBM per device.

v0:
```python
import math
import jax
import jax.numpy as jnp
from jax import lax
from jax.sharding import PartitionSpec as P


def with_halo(cells, sides, width):
    for axis, dim in sides:
        count = lax.axis_size(axis)
        ends = count - 1
        head = lax.slice_in_dim(cells, 0, width, axis=dim)
        tail = lax.slice_in_dim(cells, cells.shape[dim] - width, cells.shape[dim], axis=dim)
        cells = jnp.concatenate(
            [
                lax.ppermute(tail, axis, [(i, (i + 1) % count) for i in range(ends)]),
                cells,
                lax.ppermute(head, axis, [((i + 1) % count, i) for i in range(ends)]),
            ],
            axis=dim,
        )
    return cells


def local(
    feature_maps, query_frame, query_row, query_col, ema_decay, dw_kernel, pw_weight, out_weight
):
    frames_here, rows_here, map_width, channels = feature_maps.shape
    num_queries = query_frame.shape[0]
    first_frame = lax.axis_index("tm") * frames_here
    first_row = lax.axis_index("space") * rows_here
    map_height = rows_here * lax.axis_size("space")
    local_frame = query_frame - first_frame
    local_row = query_row - first_row
    owned = (
        (local_frame >= 0)
        & (local_frame < frames_here)
        & (local_row >= 0)
        & (local_row < rows_here)
    )
    picked = feature_maps[
        jnp.clip(local_frame, 0, frames_here - 1), jnp.clip(local_row, 0, rows_here - 1), query_col
    ]
    contrib = jnp.where(owned[:, None], picked.astype(jnp.float32), 0.0)
    query_feats = lax.psum(contrib, ("tm", "space")).astype(jnp.bfloat16)
    scale = 1.0 / math.sqrt(channels)
    col_coord = jnp.arange(map_width, dtype=jnp.int32).astype(jnp.float32) / map_width
    row_coord = (first_row + jnp.arange(rows_here, dtype=jnp.int32)).astype(
        jnp.float32
    ) / map_height
    highest_list, total_list, pos_list, feat_list = ([], [], [], [])
    frame_index = 0
    frame_map = feature_maps[frame_index].reshape(rows_here * map_width, channels)
    scores = (
        lax.dot_general(
            query_feats, frame_map, (((1,), (1,)), ((), ())), preferred_element_type=jnp.float32
        )
        * scale
    )
    highest = jnp.max(scores, axis=1)
    weights_exp = jnp.exp(scores - highest[:, None])
    highest_list.append(highest)
    total_list.append(jnp.sum(weights_exp, axis=1))
    grid = weights_exp.reshape(num_queries, rows_here, map_width)
    col_part = jnp.sum(jnp.sum(grid, axis=1) * col_coord[None, :], axis=1)
    line_portion = jnp.sum(jnp.sum(grid, axis=2) * row_coord[None, :], axis=1)
    pos_list.append(jnp.stack([col_part, line_portion], 1))
    feat_list.append(
        jnp.dot(weights_exp.astype(jnp.bfloat16), frame_map, preferred_element_type=jnp.float32)
    )
    highest = jnp.stack(highest_list)
    totals = jnp.stack(total_list)
    pos_sum = jnp.stack(pos_list)
    feat_sum = jnp.stack(feat_list)
    top_value = lax.pmax(highest, "space")
    factor = jnp.exp(highest - top_value)
    grand_total, pos_all, feat_all = lax.psum(
        (factor * totals, factor[..., None] * pos_sum, factor[..., None] * feat_sum), "space"
    )
    position = pos_all / grand_total[..., None]
    focused_result = (feat_all / grand_total[..., None]).astype(jnp.bfloat16)
    padded = with_halo(focused_result, (("tm", 0),), 1).astype(jnp.float32)
    depth = jnp.zeros((frames_here, num_queries, channels), jnp.float32)
    for tap in range(dw_kernel.shape[0]):
        depth = depth + dw_kernel[tap][None, None, :] * padded[tap : tap + frames_here]
    hidden = jax.nn.gelu(depth).astype(jnp.bfloat16)
    mixed = jnp.dot(
        hidden.reshape(-1, channels), pw_weight, preferred_element_type=jnp.float32
    ).reshape(frames_here, num_queries, channels)
    refined = focused_result.astype(jnp.float32) + mixed
    carried = jnp.zeros((num_queries, channels), jnp.float32)
    retain_prod = jnp.ones((channels,), jnp.float32)
    local_states, local_prods = ([], [])
    frame_index = 0
    retain = ema_decay[frame_index]
    carried = retain[None, :] * carried + (1.0 - retain[None, :]) * refined[frame_index]
    retain_prod = retain_prod * retain
    local_states.append(carried)
    local_prods.append(retain_prod)
    all_prods, all_ends = (
        lax.all_gather(retain_prod[None], "tm", axis=0, tiled=True),
        lax.all_gather(carried[None], "tm", axis=0, tiled=True),
    )
    position_tm = lax.axis_index("tm")

    def fold_step(source, running):
        advanced = all_prods[source][None, :] * running + all_ends[source]
        return jnp.where(source < position_tm, advanced, running)

    incoming = lax.fori_loop(
        0, lax.axis_size("tm"), fold_step, jnp.zeros((num_queries, channels), jnp.float32)
    )
    memory = jnp.stack(local_states) + jnp.stack(local_prods)[:, None, :] * incoming[None]
    delta = jnp.einsum("tqc,kc->tkq", memory, out_weight, precision=lax.Precision.HIGHEST)
    return jnp.transpose(position, (0, 2, 1)) + delta


def solution(mesh):
    placed = (
        P(("video", "tm"), "space", None, None),
        P("video"),
        P("video"),
        P("video"),
        P(("video", "tm"), None),
        P(),
        P(),
        P(),
    )
    return jax.shard_map(
        local, mesh=mesh, in_specs=placed, out_specs=P(("video", "tm"), None, None), check_vma=False
    )
```

profile of v0, /device:TPU:1, one launch (start us, length us, event | category | flops | bytes accessed | tf_op | source)
XLA Modules:
  0.0 416.0 jit_solution(9454271297745757524)
XLA Ops:
  8.1 3.1 gather_fusion
  11.4 250.4 %all-reduce.5 = bf16[512,128]{1,0:T(8,128)(2,1)S(1)} all-reduce(f32[512,128]{1,0:T(8,128)S(1)} %convert_select_fusion), channel_id=1, replica_groups=mesh['video'=4,'tm'=16,'space'=4] {'tm','space'}, use_global_device_ids=true, to_apply=%region_0.1 | all-reduce | flops 65536 | bytes 393216 | tf_op jit(solution)/shard_map/psum | solution.py:45
  261.8 2.3 multiply_reduce_fusion
  264.1 7.0 %fusion.50 = (f32[512]{0:T(512)S(1)}, f32[512,7680]{1,0:T(8,128)}) fusion(f32[512]{0:T(512)S(1)} %get-tuple-element.139, f32[512,7680]{1,0:T(8,128)S(1)} %get-tuple-element.140), kind=kLoop, calls=%fused_computation.74 | loop fusion | flops 11795968 | bytes 31461376 | tf_op jit(solution)/shard_map/reduce_sum | solution.py:63
  271.1 6.0 %pmax.7 = f32[1,512]{1,0:T(1,128)S(1)} all-reduce(f32[1,512]{1,0:T(1,128)S(1)} %bitcast.66), channel_id=1, replica_groups=mesh['video'=4,'tm'=16,'space'=4] {'space'}, use_global_device_ids=true, to_apply=%region_2.3 | all-reduce | flops 512 | bytes 4096 | tf_op jit(solution)/shard_map/pmax | solution.py:75
  277.1 8.4 %fusion.7 = f32[1,512,128]{2,1,0:T(8,128)} fusion(bf16[7680,128]{1,0:T(8,128)(2,1)S(1)} %bitcast.62, f32[512,7680]{1,0:T(8,128)} %get-tuple-element.135, f32[512]{0:T(512)S(1)} %bitcast.64), kind=kOutput, calls=%fused_computation.11 | convolution fusion | flops 1010630656 | bytes 17958912 | tf_op jit(solution)/shard_map/dot_general | solution.py:69
  285.5 15.7 %copy.10 = f32[512,7680]{0,1:T(8,128)} copy(f32[512,7680]{1,0:T(8,128)} %get-tuple-element.135) | data formatting | bytes 31457280 | tf_op jit(solution)/shard_map/exp | solution.py:61
  301.3 7.9 %fusion.48 = (f32[512,240]{0,1:T(8,128)S(1)}, f32[512,32]{0,1:T(8,128)S(1)}) fusion(f32[512,32,240]{0,2,1:T(8,128)} %bitcast.63), kind=kLoop, calls=%fused_computation.72 | loop fusion | flops 7725056 | bytes 16285696 | tf_op jit(solution)/shard_map/reduce_sum | solution.py:65
  309.4 7.5 %all-reduce = (f32[512]{0:T(512)S(1)}, f32[1,512,2]{1,2,0:T(2,128)S(1)}) all-reduce(f32[512]{0:T(512)S(1)} %bitcast.70, f32[1,512,2]{1,2,0:T(2,128)S(1)} %maximum_multiply_fusion), channel_id=1, replica_groups=mesh['video'=4,'tm'=16,'space'=4] {'space'}, use_global_device_ids=true, to_apply=%region_9.10 | all-reduce | flops 1536 | bytes 12288 | tf_op jit(solution)/shard_map/psum | solution.py:77
  317.0 15.6 %all-reduce.4.cloned.1.call-done = f32[1,512,128]{2,1,0:T(8,128)} async-done(((f32[1,512,128]{2,1,0:T(8,128)}), f32[1,512,128]{2,1,0:T(8,128)}) %all-reduce.4.cloned.1.call-update) | async-done | bytes 262160 | tf_op jit(solution)/shard_map/psum | solution.py:77
  333.7 4.7 %collective-permute-start.1 = (bf16[1,512,128]{2,1,0:T(8,128)(2,1)S(1)}, bf16[1,512,128]{2,1,0:T(8,128)(2,1)S(1)}, u32[]{:S(2)}, u32[]{:S(2)}) collective-permute-start(bf16[1,512,128]{2,1,0:T(8,128)(2,1)S(1)} %divide_convert_fusion), channel_id=1, source_target_pairs={{4,0},{8,4},{12,8},{16,12},{20,16},{24,20},{28,24},{32,28},{36,32}... | collective-permute-start | bytes 393224 | tf_op jit(solution)/shard_map/ppermute | solution.py:18
  338.4 3.1 collective-permute-start
  342.2 1.2 collective-permute-done
  344.5 18.6 %all-gather = f32[16,1,128]{2,1,0:T(1,128)S(1)} all-gather(f32[1,1,128]{2,1,0:T(1,128)S(1)} %bitcast.73), channel_id=1, replica_groups=mesh['video'=4,'tm'=16,'space'=4] {'tm'}, dimensions={0}, use_global_device_ids=true | all-gather | bytes 8704 | tf_op jit(solution)/shard_map/all_gather | solution.py:101
  363.0 26.2 %all-gather.3.cloned.1.call-done = f32[16,512,128]{2,1,0:T(8,128)} async-done(((f32[1,512,128]{2,1,0:T(8,128)}), f32[16,512,128]{2,1,0:T(8,128)}) %all-gather.3.cloned.1.call-update) | async-done | bytes 4194320 | tf_op jit(solution)/shard_map/all_gather | solution.py:102
  389.2 19.0 %while.14 = (s32[]{:T(128)}, f32[512,128]{1,0:T(8,128)S(1)}, s32[]{:T(128)}, f32[16,128]{1,0:T(8,128)S(1)}, f32[16,512,128]{2,1,0:T(8,128)}, /*index=5*/s32[]{:T(128)}, s32[]{:T(128)}) while((s32[]{:T(128)}, f32[512,128]{1,0:T(8,128)S(1)}, s32[]{:T(128)}, f32[16,128]{1,0:T(8,128)S(1)}, f32[16,512,128]{2,1,0:T(8,128)}, ...), condition=%wide.region_12.13_spmd.clone, body=%wide.region_11.12_spmd.clone.sunk | while | flops 262148 | bytes 788081 | solution.py:110
  389.2 1.1 fusion.57
  390.4 1.1 fusion.57
  391.6 1.1 fusion.57
  392.8 1.1 fusion.57
  394.0 1.1 fusion.57
  395.1 1.1 fusion.57
  396.3 1.1 fusion.57
  397.5 1.1 fusion.57
  398.7 1.1 fusion.57
  399.9 1.1 fusion.57
  401.1 1.1 fusion.57
  402.3 1.1 fusion.57
  403.5 1.1 fusion.57
  404.7 1.1 fusion.57
  405.9 1.1 fusion.57
  407.0 1.1 fusion.57
  (48 shorter events, 6.0 us)
Async XLA Ops:
  6.5 1.6 copy-start
  6.5 326.1 %all-reduce.4.cloned.1.call-start = ((), (), s32[]{:S(2)}) async-start(), calls=%async_computation | async-start | bytes 524288 | tf_op jit(solution)/shard_map/psum | solution.py:77
  285.5 103.7 %all-gather.3.cloned.1.call-start = ((), (), s32[]{:S(2)}) async-start(), calls=%async_computation.1 | async-start | bytes 4456448 | tf_op jit(solution)/shard_map/all_gather | solution.py:102
  301.3 8.1 %copy-start.1 = (f32[1,128]{1,0:T(1,128)S(1)}, f32[1,128]{1,0:T(1,128)}, u32[]{:S(2)}) copy-start(f32[1,128]{1,0:T(1,128)} %param.14) | copy-start | bytes 1540
  301.3 15.7 %copy-start.2 = (f32[3,128]{1,0:T(4,128)S(1)}, f32[3,128]{1,0:T(4,128)}, u32[]{:S(2)}) copy-start(f32[3,128]{1,0:T(4,128)} %param.15) | copy-start | bytes 4612
  301.3 42.2 %copy-start.4 = (bf16[128,128]{1,0:T(8,128)(2,1)S(1)}, bf16[128,128]{1,0:T(8,128)(2,1)}, u32[]{:S(2)}) copy-start(bf16[128,128]{1,0:T(8,128)(2,1)} %param.16) | copy-start | bytes 98308
  301.3 106.9 %copy-start.3 = (f32[2,128]{1,0:T(2,128)S(1)}, f32[2,128]{1,0:T(2,128)}, u32[]{:S(2)}) copy-start(f32[2,128]{1,0:T(2,128)} %param.17) | copy-start | bytes 3076
  333.7 8.5 %collective-permute-start.1 = (bf16[1,512,128]{2,1,0:T(8,128)(2,1)S(1)}, bf16[1,512,128]{2,1,0:T(8,128)(2,1)S(1)}, u32[]{:S(2)}, u32[]{:S(2)}) collective-permute-start(bf16[1,512,128]{2,1,0:T(8,128)(2,1)S(1)} %divide_convert_fusion), channel_id=1, source_target_pairs={{4,0},{8,4},{12,8},{16,12},{20,16},{24,20},{28,24},{32,28},{36,32}... | collective-permute-start | bytes 393224 | tf_op jit(solution)/shard_map/ppermute | solution.py:18
  338.4 5.0 %collective-permute-start = (bf16[1,512,128]{2,1,0:T(8,128)(2,1)S(1)}, bf16[1,512,128]{2,1,0:T(8,128)(2,1)S(1)}, u32[]{:S(2)}, u32[]{:S(2)}) collective-permute-start(bf16[1,512,128]{2,1,0:T(8,128)(2,1)S(1)} %divide_convert_fusion), channel_id=1, source_target_pairs={{0,4},{4,8},{8,12},{12,16},{16,20},{20,24},{24,28},{28,32},{32,36}... | collective-permute-start | bytes 393224 | tf_op jit(solution)/shard_map/ppermute | solution.py:16
Sparse Core Ops, SparseCore 0:
  285.6 46.9 all-reduce.3
  344.6 44.5 all-gather.2
where the time goes:
time: 417 us; the launch traced here: 416 us
  blocking collectives  282 us (68%)
  waiting for transfers between devices  43.7 us (10%)
  other arithmetic  36.3 us (9%)
  local copies, waits for them, and re-layouts  19 us (5%)
  between operations  13.6 us (3%)
  matrix products  12.6 us (3%)
  starting transfers between devices  7.84 us (2%)
    psum x1, blocking collectives, local(): query_feats = lax.psum(contrib, ('tm', 'space')).astype(jnp.bfloat16)  250 us
    all_gather x1, waiting for transfers between devices, local(): lax.all_gather(carried[None], 'tm', axis=0, tiled=True)  26.2 us
    all_gather x1, blocking collectives, local(): lax.all_gather(retain_prod[None], 'tm', axis=0, tiled=True)  18.6 us
    select_n x16, other arithmetic, fold_step(): return jnp.where(source < position_tm, advanced, running)  18.4 us
    exp x1, local copies, waits for them, and re-layouts, local(): weights_exp = jnp.exp(scores - highest[:, None])  15.7 us
    psum x1, waiting for transfers between devices, local(): lax.psum((factor * totals, factor[..., None] * pos_sum, factor[..., None]...  15.6 us
    dot_general x1, matrix products, local(): jnp.dot(weights_exp.astype(jnp.bfloat16), frame_map, preferred_element_ty...  8.38 us
  transfers between devices with their start and end apart: 4, of which 4 were waited for; matrix products, arithmetic and copies ran while one was open for 6% of the time, Pallas kernels for 0%

commit v1 on v0

--- a/solution.py
+++ b/solution.py
@@ -42,7 +42,7 @@
         jnp.clip(local_frame, 0, frames_here - 1), jnp.clip(local_row, 0, rows_here - 1), query_col
     ]
     contrib = jnp.where(owned[:, None], picked.astype(jnp.float32), 0.0)
-    query_feats = lax.psum(contrib, ("tm", "space")).astype(jnp.bfloat16)
+    query_feats = lax.psum(lax.psum(contrib, "space"), "tm").astype(jnp.bfloat16)
     scale = 1.0 / math.sqrt(channels)
     col_coord = jnp.arange(map_width, dtype=jnp.int32).astype(jnp.float32) / map_width
     row_coord = (first_row + jnp.arange(rows_here, dtype=jnp.int32)).astype(

time: 417 us -> 283 us (0.68)
  blocking collectives: 282 us -> 80.3 us
  waiting for transfers between devices: 43.7 us -> 110 us
    psum x1, blocking collectives: 250 us -> 48.3 us  [local(): lax.psum(lax.psum(contrib, 'space'), 'tm').astype(jnp.bfloat16)]
    psum x0 -> x1, waiting for transfers between devices: none -> 47.3 us  [local(): lax.psum(contrib, 'space')]
    psum x1, waiting for transfers between devices: 15.6 us -> 34.1 us  [local(): lax.psum((factor * totals, factor[..., None] * pos_sum, factor[..., None]...]
  transfers between devices with their start and end apart: 4 -> 5, of which waited for: 4 -> 5; matrix products, arithmetic and copies ran while one was open for 6% -> 3% of each run, Pallas kernels for 0% -> 0%
where the time goes in v1:
time: 283 us; the launch traced here: 281 us
  waiting for transfers between devices  110 us (39%)
  blocking collectives  80.3 us (28%)
  other arithmetic  37.7 us (13%)
  local copies, waits for them, and re-layouts  19.7 us (7%)
  between operations  13.3 us (5%)
  matrix products  12.6 us (4%)
  starting transfers between devices  7.88 us (3%)
    psum x1, blocking collectives, local(): lax.psum(lax.psum(contrib, 'space'), 'tm').astype(jnp.bfloat16)  48.3 us
    psum x1, waiting for transfers between devices, local(): lax.psum(contrib, 'space')  47.3 us
    psum x1, waiting for transfers between devices, local(): lax.psum((factor * totals, factor[..., None] * pos_sum, factor[..., None]...  34.1 us
    all_gather x1, waiting for transfers between devices, local(): lax.all_gather(carried[None], 'tm', axis=0, tiled=True)  26.2 us
    all_gather x1, blocking collectives, local(): lax.all_gather(retain_prod[None], 'tm', axis=0, tiled=True)  18.6 us
    select_n x16, other arithmetic, fold_step(): return jnp.where(source < position_tm, advanced, running)  18.4 us
    exp x1, local copies, waits for them, and re-layouts, local(): weights_exp = jnp.exp(scores - highest[:, None])  15.6 us
    dot_general x1, matrix products, local(): jnp.dot(weights_exp.astype(jnp.bfloat16), frame_map, preferred_element_ty...  8.38 us
  transfers between devices with their start and end apart: 5, of which 5 were waited for; matrix products, arithmetic and copies ran while one was open for 3% of the time, Pallas kernels for 0%

profile of v1, /device:TPU:1, one launch (start us, length us, event | category | flops | bytes accessed | tf_op | source)
XLA Modules:
  0.0 281.4 jit_solution(1113615117458212979)
XLA Ops:
  8.1 3.1 %gather_fusion = bf16[512,128]{1,0:T(8,128)(2,1)S(1)} fusion(bf16[1,32,240,128]{3,2,1,0:T(8,128)(2,1)S(1)} %copy-done, s32[512]{0:T(512)S(1)} %fusion.41), kind=kCustom, calls=%fused_computation | custom fusion | bytes 268288 | tf_op jit(solution)/shard_map/gather | solution.py:41
  13.6 47.3 %all-reduce.5.cloned.1.call-done = f32[512,128]{1,0:T(8,128)} async-done(((f32[512,128]{1,0:T(8,128)}), f32[512,128]{1,0:T(8,128)}) %all-reduce.5.cloned.1.call-update) | async-done | bytes 262160 | tf_op jit(solution)/shard_map/psum | solution.py:45
  60.9 48.3 %all-reduce.8 = bf16[512,128]{1,0:T(8,128)(2,1)S(1)} all-reduce(f32[512,128]{1,0:T(8,128)} %all-reduce.5.cloned.1.call-done), channel_id=1, replica_groups=mesh['video'=4,'tm'=16,'space'=4] {'tm'}, use_global_device_ids=true, to_apply=%region_1.2 | all-reduce | flops 65536 | bytes 393216 | tf_op jit(solution)/shard_map/psum | solution.py:45
  109.2 2.3 multiply_reduce_fusion
  111.5 7.0 %fusion.50 = (f32[512]{0:T(512)S(1)}, f32[512,7680]{1,0:T(8,128)}) fusion(f32[512]{0:T(512)S(1)} %get-tuple-element.139, f32[512,7680]{1,0:T(8,128)S(1)} %get-tuple-element.140), kind=kLoop, calls=%fused_computation.74 | loop fusion | flops 11795968 | bytes 31461376 | tf_op jit(solution)/shard_map/reduce_sum | solution.py:63
  118.5 7.4 %pmax.7 = f32[1,512]{1,0:T(1,128)S(1)} all-reduce(f32[1,512]{1,0:T(1,128)S(1)} %bitcast.66), channel_id=1, replica_groups=mesh['video'=4,'tm'=16,'space'=4] {'space'}, use_global_device_ids=true, to_apply=%region_3.4 | all-reduce | flops 512 | bytes 4096 | tf_op jit(solution)/shard_map/pmax | solution.py:75
  125.9 15.6 %copy.10 = f32[512,7680]{0,1:T(8,128)} copy(f32[512,7680]{1,0:T(8,128)} %get-tuple-element.135) | data formatting | bytes 31457280 | tf_op jit(solution)/shard_map/exp | solution.py:61
  141.6 8.4 %fusion.7 = f32[1,512,128]{2,1,0:T(8,128)} fusion(bf16[7680,128]{1,0:T(8,128)(2,1)S(1)} %bitcast.62, f32[512,7680]{1,0:T(8,128)} %get-tuple-element.135, f32[512]{0:T(512)S(1)} %bitcast.64), kind=kOutput, calls=%fused_computation.11 | convolution fusion | flops 1010630656 | bytes 17958912 | tf_op jit(solution)/shard_map/dot_general | solution.py:69
  150.0 7.8 %fusion.48 = (f32[512,240]{0,1:T(8,128)S(1)}, f32[512,32]{0,1:T(8,128)S(1)}) fusion(f32[512,32,240]{0,2,1:T(8,128)} %bitcast.63), kind=kLoop, calls=%fused_computation.72 | loop fusion | flops 7725056 | bytes 16285696 | tf_op jit(solution)/shard_map/reduce_sum | solution.py:65
  158.1 6.1 %all-reduce = (f32[512]{0:T(512)S(1)}, f32[1,512,2]{1,2,0:T(2,128)S(1)}) all-reduce(f32[512]{0:T(512)S(1)} %bitcast.70, f32[1,512,2]{1,2,0:T(2,128)S(1)} %maximum_multiply_fusion), channel_id=1, replica_groups=mesh['video'=4,'tm'=16,'space'=4] {'space'}, use_global_device_ids=true, to_apply=%region_10.11 | all-reduce | flops 1536 | bytes 12288 | tf_op jit(solution)/shard_map/psum | solution.py:77
  164.2 34.1 %all-reduce.7.cloned.1.call-done = f32[1,512,128]{2,1,0:T(8,128)} async-done(((f32[1,512,128]{2,1,0:T(8,128)}), f32[1,512,128]{2,1,0:T(8,128)}) %all-reduce.7.cloned.1.call-update) | async-done | bytes 262160 | tf_op jit(solution)/shard_map/psum | solution.py:77
  199.4 4.7 %collective-permute-start.1 = (bf16[1,512,128]{2,1,0:T(8,128)(2,1)S(1)}, bf16[1,512,128]{2,1,0:T(8,128)(2,1)S(1)}, u32[]{:S(2)}, u32[]{:S(2)}) collective-permute-start(bf16[1,512,128]{2,1,0:T(8,128)(2,1)S(1)} %divide_convert_fusion), channel_id=1, source_target_pairs={{4,0},{8,4},{12,8},{16,12},{20,16},{24,20},{28,24},{32,28},{36,32}... | collective-permute-start | bytes 393224 | tf_op jit(solution)/shard_map/ppermute | solution.py:18
  204.1 3.1 %collective-permute-start = (bf16[1,512,128]{2,1,0:T(8,128)(2,1)S(1)}, bf16[1,512,128]{2,1,0:T(8,128)(2,1)S(1)}, u32[]{:S(2)}, u32[]{:S(2)}) collective-permute-start(bf16[1,512,128]{2,1,0:T(8,128)(2,1)S(1)} %divide_convert_fusion), channel_id=1, source_target_pairs={{0,4},{4,8},{8,12},{12,16},{16,20},{20,24},{24,28},{28,32},{32,36}... | collective-permute-start | bytes 393224 | tf_op jit(solution)/shard_map/ppermute | solution.py:16
  207.9 1.2 collective-permute-done
  210.2 18.6 %all-gather = f32[16,1,128]{2,1,0:T(1,128)S(1)} all-gather(f32[1,1,128]{2,1,0:T(1,128)S(1)} %bitcast.73), channel_id=1, replica_groups=mesh['video'=4,'tm'=16,'space'=4] {'tm'}, dimensions={0}, use_global_device_ids=true | all-gather | bytes 8704 | tf_op jit(solution)/shard_map/all_gather | solution.py:101
  228.8 26.2 %all-gather.3.cloned.1.call-done = f32[16,512,128]{2,1,0:T(8,128)} async-done(((f32[1,512,128]{2,1,0:T(8,128)}), f32[16,512,128]{2,1,0:T(8,128)}) %all-gather.3.cloned.1.call-update) | async-done | bytes 4194320 | tf_op jit(solution)/shard_map/all_gather | solution.py:102
  254.9 19.0 %while.14 = (s32[]{:T(128)}, f32[512,128]{1,0:T(8,128)S(1)}, s32[]{:T(128)}, f32[16,128]{1,0:T(8,128)S(1)}, f32[16,512,128]{2,1,0:T(8,128)}, /*index=5*/s32[]{:T(128)}, s32[]{:T(128)}) while((s32[]{:T(128)}, f32[512,128]{1,0:T(8,128)S(1)}, s32[]{:T(128)}, f32[16,128]{1,0:T(8,128)S(1)}, f32[16,512,128]{2,1,0:T(8,128)}, ...), condition=%wide.region_13.14_spmd.clone, body=%wide.region_12.13_spmd.clone.sunk | while | flops 262148 | bytes 788081 | solution.py:110
  256.1 1.1 fusion.57
  257.3 1.1 fusion.57
  258.5 1.1 fusion.57
  259.7 1.1 fusion.57
  260.9 1.1 fusion.57
  262.1 1.1 fusion.57
  263.3 1.1 fusion.57
  264.4 1.1 fusion.57
  265.6 1.1 fusion.57
  266.8 1.1 fusion.57
  268.0 1.1 fusion.57
  269.2 1.1 fusion.57
  270.4 1.1 fusion.57
  271.6 1.1 fusion.57
  272.8 1.1 fusion.57
  (49 shorter events, 9.3 us)
Async XLA Ops:
  6.5 1.6 copy-start
  6.5 54.4 %all-reduce.5.cloned.1.call-start = ((), (), s32[]{:S(2)}) async-start(), calls=%async_computation | async-start | bytes 524288 | tf_op jit(solution)/shard_map/psum | solution.py:45
  12.1 186.2 %all-reduce.7.cloned.1.call-start = ((), (), s32[]{:S(2)}) async-start(), calls=%async_computation.1 | async-start | bytes 524288 | tf_op jit(solution)/shard_map/psum | solution.py:77
  141.5 65.7 %copy-start.1 = (f32[1,128]{1,0:T(1,128)S(1)}, f32[1,128]{1,0:T(1,128)}, u32[]{:S(2)}) copy-start(f32[1,128]{1,0:T(1,128)} %param.14) | copy-start | bytes 1540
  141.5 67.7 %copy-start.3 = (bf16[128,128]{1,0:T(8,128)(2,1)S(1)}, bf16[128,128]{1,0:T(8,128)(2,1)}, u32[]{:S(2)}) copy-start(bf16[128,128]{1,0:T(8,128)(2,1)} %param.16) | copy-start | bytes 98308
  149.9 124.0 %copy-start.2 = (f32[2,128]{1,0:T(2,128)S(1)}, f32[2,128]{1,0:T(2,128)}, u32[]{:S(2)}) copy-start(f32[2,128]{1,0:T(2,128)} %param.17) | copy-start | bytes 3076
  150.0 105.0 %all-gather.3.cloned.1.call-start = ((), (), s32[]{:S(2)}) async-start(), calls=%async_computation.2 | async-start | bytes 4456448 | tf_op jit(solution)/shard_map/all_gather | solution.py:102
  199.4 8.5 %collective-permute-start.1 = (bf16[1,512,128]{2,1,0:T(8,128)(2,1)S(1)}, bf16[1,512,128]{2,1,0:T(8,128)(2,1)S(1)}, u32[]{:S(2)}, u32[]{:S(2)}) collective-permute-start(bf16[1,512,128]{2,1,0:T(8,128)(2,1)S(1)} %divide_convert_fusion), channel_id=1, source_target_pairs={{4,0},{8,4},{12,8},{16,12},{20,16},{24,20},{28,24},{32,28},{36,32}... | collective-permute-start | bytes 393224 | tf_op jit(solution)/shard_map/ppermute | solution.py:18
  204.1 5.0 %collective-permute-start = (bf16[1,512,128]{2,1,0:T(8,128)(2,1)S(1)}, bf16[1,512,128]{2,1,0:T(8,128)(2,1)S(1)}, u32[]{:S(2)}, u32[]{:S(2)}) collective-permute-start(bf16[1,512,128]{2,1,0:T(8,128)(2,1)S(1)} %divide_convert_fusion), channel_id=1, source_target_pairs={{0,4},{4,8},{8,12},{12,16},{16,20},{20,24},{24,28},{28,32},{32,36}... | collective-permute-start | bytes 393224 | tf_op jit(solution)/shard_map/ppermute | solution.py:16
Sparse Core Ops, SparseCore 0:
  12.2 48.6 all-reduce.4
  150.1 48.1 all-reduce.6
  210.3 44.5 all-gather.2
